TPU v7x, 128 devices: a whole 4x4x4 slice. The times are simulated.
128 devices in a mesh: dp: 64 (over z, y_lo, x, core), mp: 2 (over y_hi).
Axes of the slice: x: 4, y: 4 (y_hi: 2, y_lo: 2; y = y_hi * 2 + y_lo), z: 4, core: 2. Of those that a mesh axis runs over, the one named last changes fastest.
Arguments:
- images: bfloat16 [128, 197, 384], P('dp'), may hold values from -6 to 6
- routes: int32 [1, 128, 197, 2], P(None, 'dp'), may hold values from 0 to 3, all different within a row; in each aligned block of 197 rows (0 to 196, 197 to 393, ..., all dimensions but the last counted through in order) at most 104 rows name the same one
- w_qkv: bfloat16 [1, 384, 3, 384], P(None, 'dp', None, 'mp'), may hold values from -0.3125 to 0.3125
- w_proj: bfloat16 [1, 384, 384], P(None, 'mp', 'dp'), may hold values from -2 to 2
- w_in: bfloat16 [1, 4, 384, 1536], P(None, None, 'dp', 'mp'), may hold values from -0.3125 to 0.3125
- w_out: bfloat16 [1, 4, 1536, 384], P(None, None, 'mp', 'dp'), may hold values from -0.3125 to 0.3125
- w_router: bfloat16 [1, 384, 4], P(None, 'dp'), may hold values from -0.625 to 0.625
- ln_gain: bfloat16 [1, 2, 384], P(None, None, 'dp'), may hold values from 0.5 to 1.5
- ln_bias: bfloat16 [1, 2, 384], P(None, None, 'dp'), may hold values from -3 to 3
- cotangent: bfloat16 [128, 197, 384], P('dp'), may hold values from -6 to 6
Outputs:
- activations: float32 [128, 197, 384], P('dp')
- grad_images: float32 [128, 197, 384], P('dp')
- grad_qkv: float32 [1, 384, 3, 384], P(None, 'dp', None, 'mp')
- grad_proj: float32 [1, 384, 384], P(None, 'mp', 'dp')
- grad_in: float32 [1, 4, 384, 1536], P(None, None, 'dp', 'mp')
- grad_out: float32 [1, 4, 1536, 384], P(None, None, 'mp', 'dp')
- grad_router: float32 [1, 384, 4], P(None, 'dp')
- grad_gain: float32 [1, 2, 384], P(None, None, 'dp')
- grad_bias: float32 [1, 2, 384], P(None, None, 'dp')
Inputs may be any that keep to these rules, and one draw needn't show every extreme that they name: `routes`: in each block, each aligned group of 1 images names every expert in at most 104 of its tokens, and some group names some expert in exactly 104; a token's two experts differ.
All inputs are finite; a program needn't handle non-finite values.
Results may differ from a plain program's by a relative error of at most 0.024.
Values may be sent and summed in bfloat16 or wider, within the bound.
A program may use at most 128 MiB of HBM per device.

v0:
```python
import jax
import jax.numpy as jnp
from jax import lax
from jax.sharding import PartitionSpec as P

HD = 64
EXPERTS = 4
TOPK = 2
LAYERS = 1
MICRO = 2
IMG_MB = 1
CAP = 104
EPSILON = 1e-06


def norm_forward(field, gain_row, shift_row):
    mean_value = jnp.mean(field, axis=-1, keepdims=True)
    centered = field - mean_value
    inverse = lax.rsqrt(jnp.mean(centered * centered, axis=-1, keepdims=True) + EPSILON)
    normed = centered * inverse
    return (normed * gain_row + shift_row, normed, inverse)


def norm_backward(grad_out, normed, inverse, gain_row):
    grad_gain = jnp.sum(grad_out * normed, axis=0)
    grad_shift = jnp.sum(grad_out, axis=0)
    scaled = grad_out * gain_row
    grad_in = inverse * (
        scaled
        - jnp.mean(scaled, axis=-1, keepdims=True)
        - normed * jnp.mean(scaled * normed, axis=-1, keepdims=True)
    )
    return (grad_in, grad_gain, grad_shift)


def slot_positions(chosen_ids):
    labels = jnp.arange(EXPERTS, dtype=jnp.int32)
    hit_counts = jnp.sum((chosen_ids[:, :, None] == labels).astype(jnp.int32), axis=1)
    before = jnp.cumsum(hit_counts, axis=0) - hit_counts
    return jnp.take_along_axis(before, chosen_ids, axis=1)


def gelu_slope(inner_pre):
    cumulative = 0.5 * (1.0 + jax.scipy.special.erf(inner_pre * 0.7071067811865476))
    density = jnp.exp(-0.5 * inner_pre * inner_pre) * 0.3989422804014327
    return cumulative + inner_pre * density


def fetch_layer(layer_index, w_qkv, w_proj, w_in, w_out, w_router, ln_gain, ln_bias):
    return (
        lax.all_gather(w_qkv[layer_index], "dp", axis=0, tiled=True),
        lax.all_gather(w_proj[layer_index], "dp", axis=1, tiled=True),
        lax.all_gather(w_in[layer_index], "dp", axis=1, tiled=True),
        lax.all_gather(w_out[layer_index], "dp", axis=2, tiled=True),
        lax.all_gather(w_router[layer_index], "dp", axis=0, tiled=True),
        lax.all_gather(ln_gain[layer_index], "dp", axis=1, tiled=True),
        lax.all_gather(ln_bias[layer_index], "dp", axis=1, tiled=True),
    )


def layer_forward(field, chosen_ids, weights):
    w_qkv, w_proj, w_in, w_out, w_router, ln_gain, ln_bias = weights
    image_count, length, model_width = field.shape
    row_count = image_count * length
    head_count = w_qkv.shape[2] // HD
    score_scale = HD ** (-0.5)
    gain_rows = ln_gain.astype(jnp.float32)
    shift_rows = ln_bias.astype(jnp.float32)
    flat = field.reshape(row_count, model_width)
    first, normed_one, inverse_one = norm_forward(flat, gain_rows[0], shift_rows[0])
    first = first.astype(jnp.bfloat16)
    projected = jnp.einsum("rd,dcf->rcf", first, w_qkv, preferred_element_type=jnp.float32).astype(
        jnp.bfloat16
    )
    projected = projected.reshape(image_count, length, 3, head_count, HD)
    queries = projected[:, :, 0]
    key_rows = projected[:, :, 1]
    value_rows = projected[:, :, 2]
    scores = (
        jnp.einsum("bqhe,bkhe->bhqk", queries, key_rows, preferred_element_type=jnp.float32)
        * score_scale
    )
    log_total = jax.nn.logsumexp(scores, axis=-1)
    attn_weights = jnp.exp(scores - log_total[..., None]).astype(jnp.bfloat16)
    attended = jnp.einsum(
        "bhqk,bkhe->bqhe", attn_weights, value_rows, preferred_element_type=jnp.float32
    )
    attended = attended.astype(jnp.bfloat16).reshape(row_count, head_count * HD)
    partial_attn = jnp.dot(attended, w_proj, preferred_element_type=jnp.float32)
    hidden = flat + lax.psum(partial_attn, "mp")
    second, normed_two, inverse_two = norm_forward(hidden, gain_rows[1], shift_rows[1])
    second = second.astype(jnp.bfloat16)
    logits = jnp.dot(second, w_router, preferred_element_type=jnp.float32)
    router = jax.nn.softmax(logits, axis=-1)
    labels = jnp.arange(EXPERTS, dtype=jnp.int32)
    chosen = (chosen_ids[:, :, None] == labels).astype(jnp.float32)
    gate_values = jnp.sum(router[:, None, :] * chosen, axis=-1)
    slot_index = (chosen_ids * CAP + slot_positions(chosen_ids)).reshape(-1)
    owners = (
        jnp.full((EXPERTS * CAP,), row_count, jnp.int32)
        .at[slot_index]
        .set(jnp.repeat(jnp.arange(row_count, dtype=jnp.int32), TOPK))
    )
    slot_gate = jnp.zeros((EXPERTS * CAP,), jnp.float32).at[slot_index].set(gate_values.reshape(-1))
    padded = jnp.concatenate([second, jnp.zeros((1, model_width), jnp.bfloat16)], axis=0)
    slot_rows = jnp.take(padded, owners, axis=0).reshape(EXPERTS, CAP, model_width)
    inner_pre = jnp.einsum("ecd,edf->ecf", slot_rows, w_in, preferred_element_type=jnp.float32)
    activated = jax.nn.gelu(inner_pre, approximate=False).astype(jnp.bfloat16)
    produced = jnp.einsum("ecf,efd->ecd", activated, w_out, preferred_element_type=jnp.float32)
    produced = produced.reshape(EXPERTS * CAP, model_width)
    picked = jnp.take(produced, slot_index, axis=0).reshape(row_count, TOPK, model_width)
    partial_moe = jnp.sum(gate_values[:, :, None] * picked, axis=1)
    output = hidden + lax.psum(partial_moe.astype(jnp.bfloat16), "mp").astype(jnp.float32)
    record = (
        normed_one,
        inverse_one,
        first,
        projected,
        log_total,
        attended,
        normed_two,
        inverse_two,
        second,
        router,
        chosen,
        slot_index,
        owners,
        slot_gate,
        slot_rows,
        inner_pre,
        activated,
        picked,
    )
    return (output.reshape(image_count, length, model_width), record)


def layer_backward(grad_field, record, weights):
    w_qkv, w_proj, w_in, w_out, w_router, ln_gain, ln_bias = weights
    (
        normed_one,
        inverse_one,
        first,
        projected,
        log_total,
        attended,
        normed_two,
        inverse_two,
        second,
        router,
        chosen,
        slot_index,
        owners,
        slot_gate,
        slot_rows,
        inner_pre,
        activated,
        picked,
    ) = record
    image_count, length, model_width = grad_field.shape
    row_count = image_count * length
    head_count = projected.shape[3]
    score_scale = HD ** (-0.5)
    gain_rows = ln_gain.astype(jnp.float32)
    grad_flat = grad_field.reshape(row_count, model_width)
    padded_grad = jnp.concatenate([grad_flat, jnp.zeros((1, model_width), jnp.float32)], axis=0)
    grad_slots = (jnp.take(padded_grad, owners, axis=0) * slot_gate[:, None]).astype(jnp.bfloat16)
    grad_slots = grad_slots.reshape(EXPERTS, CAP, model_width)
    grad_w_out = jnp.einsum(
        "ecf,ecd->efd", activated, grad_slots, preferred_element_type=jnp.float32
    )
    grad_act = jnp.einsum("ecd,efd->ecf", grad_slots, w_out, preferred_element_type=jnp.float32)
    grad_inner = (grad_act * gelu_slope(inner_pre)).astype(jnp.bfloat16)
    grad_w_in = jnp.einsum(
        "ecd,ecf->edf", slot_rows, grad_inner, preferred_element_type=jnp.float32
    )
    grad_slot_rows = jnp.einsum(
        "ecf,edf->ecd", grad_inner, w_in, preferred_element_type=jnp.float32
    )
    grad_slot_rows = grad_slot_rows.reshape(EXPERTS * CAP, model_width)
    partial_second = jnp.sum(
        jnp.take(grad_slot_rows, slot_index, axis=0).reshape(row_count, TOPK, model_width), axis=1
    )
    partial_gate = jnp.sum(picked * grad_flat[:, None, :], axis=-1)
    grad_second, grad_gate = lax.psum((partial_second, partial_gate), "mp")
    grad_router = jnp.sum(grad_gate[:, :, None] * chosen, axis=1)
    grad_logits = router * (grad_router - jnp.sum(router * grad_router, axis=-1, keepdims=True))
    grad_logits = grad_logits.astype(jnp.bfloat16)
    grad_w_router = jnp.dot(second.T, grad_logits, preferred_element_type=jnp.float32)
    grad_second = grad_second + jnp.dot(grad_logits, w_router.T, preferred_element_type=jnp.float32)
    grad_from_norm, grad_gain_two, grad_shift_two = norm_backward(
        grad_second, normed_two, inverse_two, gain_rows[1]
    )
    grad_hidden = grad_flat + grad_from_norm
    grad_hidden_low = grad_hidden.astype(jnp.bfloat16)
    grad_w_proj = jnp.dot(attended.T, grad_hidden_low, preferred_element_type=jnp.float32)
    grad_attended = jnp.dot(grad_hidden_low, w_proj.T, preferred_element_type=jnp.float32).astype(
        jnp.bfloat16
    )
    grad_attended = grad_attended.reshape(image_count, length, head_count, HD)
    queries = projected[:, :, 0]
    key_rows = projected[:, :, 1]
    value_rows = projected[:, :, 2]
    scores = (
        jnp.einsum("bqhe,bkhe->bhqk", queries, key_rows, preferred_element_type=jnp.float32)
        * score_scale
    )
    probs = jnp.exp(scores - log_total[..., None])
    grad_values = jnp.einsum(
        "bhqk,bqhe->bkhe",
        probs.astype(jnp.bfloat16),
        grad_attended,
        preferred_element_type=jnp.float32,
    )
    grad_probs = jnp.einsum(
        "bqhe,bkhe->bhqk", grad_attended, value_rows, preferred_element_type=jnp.float32
    )
    grad_scores = (
        probs * (grad_probs - jnp.sum(probs * grad_probs, axis=-1, keepdims=True))
    ).astype(jnp.bfloat16)
    grad_queries = (
        jnp.einsum("bhqk,bkhe->bqhe", grad_scores, key_rows, preferred_element_type=jnp.float32)
        * score_scale
    )
    grad_keys = (
        jnp.einsum("bhqk,bqhe->bkhe", grad_scores, queries, preferred_element_type=jnp.float32)
        * score_scale
    )
    grad_projected = jnp.stack([grad_queries, grad_keys, grad_values], axis=2).astype(jnp.bfloat16)
    grad_projected = grad_projected.reshape(row_count, 3, head_count * HD)
    grad_w_qkv = jnp.einsum(
        "rd,rcf->dcf", first, grad_projected, preferred_element_type=jnp.float32
    )
    partial_first = jnp.einsum(
        "rcf,dcf->rd", grad_projected, w_qkv, preferred_element_type=jnp.float32
    )
    grad_first = lax.psum(partial_first.astype(jnp.bfloat16), "mp").astype(jnp.float32)
    grad_input_norm, grad_gain_one, grad_shift_one = norm_backward(
        grad_first, normed_one, inverse_one, gain_rows[0]
    )
    grad_input = grad_hidden + grad_input_norm
    grads = (
        grad_w_qkv,
        grad_w_proj,
        grad_w_in,
        grad_w_out,
        grad_w_router,
        jnp.stack([grad_gain_one, grad_gain_two]),
        jnp.stack([grad_shift_one, grad_shift_two]),
    )
    return (grad_input.reshape(image_count, length, model_width), grads)


def local(images, routes, w_qkv, w_proj, w_in, w_out, w_router, ln_gain, ln_bias, cotangent):
    outputs = []
    grad_parts = []
    totals = []
    for micro_index in range(MICRO):
        start_row = micro_index * IMG_MB
        field = images[start_row : start_row + IMG_MB].astype(jnp.float32)
        fetched = []
        layer_index = 0
        weights = fetch_layer(layer_index, w_qkv, w_proj, w_in, w_out, w_router, ln_gain, ln_bias)
        layer_routes = routes[layer_index, start_row : start_row + IMG_MB].reshape(-1, TOPK)
        field, record = layer_forward(field, layer_routes, weights)
        records = [record]
        fetched.append(weights)
        outputs.append(field)
        grad_field = cotangent[start_row : start_row + IMG_MB].astype(jnp.float32)
        layer_grads = [None] * LAYERS
        for layer_index in reversed(range(LAYERS)):
            weights = fetch_layer(
                layer_index, w_qkv, w_proj, w_in, w_out, w_router, ln_gain, ln_bias
            )
            grad_field, grads = layer_backward(grad_field, records[layer_index], weights)
            layer_grads[layer_index] = grads
        grad_parts.append(grad_field)
        if micro_index == 0:
            totals = layer_grads
        else:
            totals = [
                jax.tree.map(jnp.add, earlier, later) for earlier, later in zip(totals, layer_grads)
            ]
    layer_index = 0
    held = totals[layer_index]
    shards = [
        (
            lax.psum_scatter(held[0], "dp", scatter_dimension=0, tiled=True),
            lax.psum_scatter(held[1], "dp", scatter_dimension=1, tiled=True),
            lax.psum_scatter(held[2], "dp", scatter_dimension=1, tiled=True),
            lax.psum_scatter(held[3], "dp", scatter_dimension=2, tiled=True),
            lax.psum_scatter(held[4], "dp", scatter_dimension=0, tiled=True),
            lax.psum_scatter(held[5], "dp", scatter_dimension=1, tiled=True),
            lax.psum_scatter(held[6], "dp", scatter_dimension=1, tiled=True),
        )
    ]
    return (
        jnp.concatenate(outputs, axis=0),
        jnp.concatenate(grad_parts, axis=0),
        jnp.stack([piece[0] for piece in shards]),
        jnp.stack([piece[1] for piece in shards]),
        jnp.stack([piece[2] for piece in shards]),
        jnp.stack([piece[3] for piece in shards]),
        jnp.stack([piece[4] for piece in shards]),
        jnp.stack([piece[5] for piece in shards]),
        jnp.stack([piece[6] for piece in shards]),
    )


def solution(mesh):
    in_specs = (
        P("dp", None, None),
        P(None, "dp", None, None),
        P(None, "dp", None, "mp"),
        P(None, "mp", "dp"),
        P(None, None, "dp", "mp"),
        P(None, None, "mp", "dp"),
        P(None, "dp", None),
        P(None, None, "dp"),
        P(None, None, "dp"),
        P("dp", None, None),
    )
    out_specs = (
        P("dp", None, None),
        P("dp", None, None),
        P(None, "dp", None, "mp"),
        P(None, "mp", "dp"),
        P(None, None, "dp", "mp"),
        P(None, None, "mp", "dp"),
        P(None, "dp", None),
        P(None, None, "dp"),
        P(None, None, "dp"),
    )
    return jax.shard_map(local, mesh=mesh, in_specs=in_specs, out_specs=out_specs, check_vma=False)
```

profile of v0, /device:TPU:0, one launch (start us, length us, event | category | flops | bytes accessed | tf_op | source)
XLA Modules:
  0.0 1335.0 jit_solution(13719838613397084062)
XLA Ops:
  10.3 83.9 %all-gather.1 = bf16[1,2,384]{1,0,2:T(2,128)(2,1)S(1)} all-gather(bf16[1,2,6]{1,0,2:T(2,128)(2,1)S(1)} %copy.153), channel_id=3, replica_groups=mesh['dp'=64,'mp'=2] {'dp'}, dimensions={2}, use_global_device_ids=true | all-gather | bytes 1560 | tf_op jit(solution)/shard_map/all_gather | solution.py:57
  94.4 1.7 slice_reduce_fusion
  96.1 77.0 %all-gather = bf16[1,2,384]{1,0,2:T(2,128)(2,1)S(1)} all-gather(bf16[1,2,6]{1,0,2:T(2,128)(2,1)S(1)} %copy.152), channel_id=2, replica_groups=mesh['dp'=64,'mp'=2] {'dp'}, dimensions={2}, use_global_device_ids=true | all-gather | bytes 1560 | tf_op jit(solution)/shard_map/all_gather | solution.py:56
  173.3 1.7 slice_reduce_fusion.1
  175.1 78.9 %all-gather.3 = bf16[1,192,384]{1,0,2:T(2,128)(2,1)S(1)} all-gather(bf16[1,192,6]{1,0,2:T(2,128)(2,1)S(1)} %copy.157), channel_id=5, replica_groups=mesh['dp'=64,'mp'=2] {'dp'}, dimensions={2}, use_global_device_ids=true | all-gather | bytes 149760 | tf_op jit(solution)/shard_map/all_gather | solution.py:52
  255.8 78.6 %all-gather.2 = bf16[1,384,3,192]{3,2,0,1:T(4,128)(2,1)S(1)} all-gather(bf16[1,6,3,192]{3,2,0,1:T(4,128)(2,1)S(1)} %bitcast.432), channel_id=4, replica_groups=mesh['dp'=64,'mp'=2] {'dp'}, dimensions={1}, use_global_device_ids=true | all-gather | bytes 449280 | tf_op jit(solution)/shard_map/all_gather | solution.py:51
  343.7 5.9 gather_fusion.3
  353.3 5.9 gather_fusion
  360.4 2.9 scatter_custom_fusion
  363.4 2.9 scatter_custom_fusion.1
  368.4 78.4 %all-gather.4 = bf16[1,384,4]{2,0,1:T(2,128)(2,1)S(1)} all-gather(bf16[1,6,4]{2,0,1:T(2,128)(2,1)S(1)} %copy.161), channel_id=6, replica_groups=mesh['dp'=64,'mp'=2] {'dp'}, dimensions={1}, use_global_device_ids=true | all-gather | bytes 3120 | tf_op jit(solution)/shard_map/all_gather | solution.py:55
  449.9 2.6 gather_fusion.6
  452.5 2.2 gather_fusion.8
  456.8 2.2 gather_fusion.4
  459.0 2.2 gather_fusion.1
  463.9 2.6 fusion.91
  467.6 2.9 fusion.35
  470.5 85.3 %all-gather.12.cloned.1.call-done = bf16[1,4,768,384]{2,1,0,3:T(4,128)(2,1)} async-done(((bf16[1,4,768,6]{2,1,0,3:T(4,128)(2,1)}), bf16[1,4,768,384]{2,1,0,3:T(4,128)(2,1)}) %all-gather.12.cloned.1.call-update) | async-done | bytes 2359312 | tf_op jit(solution)/shard_map/all_gather | solution.py:54
  555.9 5.4 copy.169
  561.2 2.2 fusion.7
  563.5 2.2 gather_fusion.2
  565.7 2.1 multiply_reduce_fusion.3
  568.0 2.7 fusion.92
  570.7 2.9 fusion.38
  574.2 2.4 gather_fusion.5
  576.6 2.9 multiply_reduce_fusion.1
  581.0 15.0 %all-reduce.16 = (f32[197,2]{1,0:T(8,128)}, f32[197,2]{1,0:T(8,128)}) all-reduce(f32[197,2]{1,0:T(8,128)} %reduce_sum.430, f32[197,2]{1,0:T(8,128)S(1)} %reduce_sum.420), channel_id=1, replica_groups=mesh['dp'=64,'mp'=2] {'mp'}, use_global_device_ids=true, to_apply=%region_49.54 | all-reduce | flops 788 | bytes 6304 | tf_op jit(solution)/shard_map/psum | solution.py:184
  599.8 3.6 scatter_custom_fusion.2
  604.2 4.1 fusion.30
  608.3 2.9 fusion.176
  611.3 2.3 reshape.558
  613.6 1.6 copy.185
  615.1 2.5 multiply_reduce_fusion.5
  620.5 3.6 scatter_custom_fusion.3
  625.0 4.1 fusion.27
  630.3 2.6 multiply_reduce_fusion.4
  632.9 4.1 fusion.175
  637.9 2.4 gather_fusion.7
  642.7 2.5 reduce_sum.418
  645.2 2.7 fusion.9
  647.9 2.2 gather_fusion.9
  652.6 2.5 reduce_sum.428
  655.4 5.7 convolution_add_fusion.1
  661.0 30.0 %all-reduce.27.cloned.1.call-done = (f32[197,384]{1,0:T(8,128)}, f32[197,384]{1,0:T(8,128)}) async-done(((f32[197,384]{1,0:T(8,128)}, f32[197,384]{1,0:T(8,128)}), (f32[197,384]{1,0:T(8,128)}, f32[197,384]{1,0:T(8,128)})) %all-reduce.27.cloned.1.call-update) | async-done | bytes 605200 | tf_op jit(solution)/shard_map/psum | solution.py:184
  691.1 2.0 multiply_reduce_fusion.7
  693.1 2.1 multiply_reduce_fusion.6
  701.7 3.2 convolution_add_fusion
  704.9 7.5 copy.189
  712.4 5.2 copy.190
  718.6 1.5 convolution_add_fusion.2
  721.7 145.4 %fusion = f32[192,8]{0,1:T(8,128)S(1)} fusion(f32[192,384]{0,1:T(8,128)S(1)} %convolution_add_fusion.3), kind=kCustom, calls=%all-reduce-scatter | all-reduce-scatter fusion | flops 98305 | bytes 301568
  876.8 9.5 collective-permute-start.9
  886.4 2.2 collective-permute-start.8
  888.5 2.4 collective-permute-start.7
  891.0 3.8 collective-permute-start.6
  894.8 1.9 collective-permute-start.5
  896.9 2.5 collective-permute-start.4
  899.4 4.3 collective-permute-start.3
  903.7 1.6 collective-permute-start.2
  905.3 2.5 collective-permute-start.1
  907.8 2.9 collective-permute-start
  918.6 276.1 %all-reduce.14 = (f32[384,4]{0,1:T(4,128)S(1)}, f32[2,384]{1,0:T(2,128)S(1)}, f32[2,384]{1,0:T(2,128)S(1)}) all-reduce(f32[384,4]{0,1:T(4,128)S(1)} %convolution_add_fusion.6, f32[2,384]{1,0:T(2,128)S(1)} %maximum_add_fusion, f32[2,384]{1,0:T(2,128)S(1)} %maximum_add_fusion.1), channel_id=13, replica_groups=mesh['dp'=64,'mp'=2] {'dp'}, use_global_device_ids=true, to_apply=%region_62.67.clone | all-reduce | flops 3072 | bytes 24576
  1196.6 126.3 %all-reduce.25.cloned.1.call-done = (f32[384,3,192]{2,0,1:T(8,128)}, f32[4,384,768]{2,0,1:T(4,128)}, f32[4,768,384]{1,0,2:T(4,128)}) async-done(((f32[384,3,192]{2,0,1:T(8,128)}, f32[4,384,768]{2,0,1:T(4,128)}, f32[4,768,384]{1,0,2:T(4,128)}), (f32[384,3,192]{2,0,1:T(8,128)}, f32[4,384,768]{2,0,1:T(4,128)}, f32[4,768,384]{1,0,2:T(4,128)})) %all-reduce.25.cloned.1.call-update) | async-done | bytes 10321936
  1325.9 1.5 dynamic-slice_bitcast_fusion
  (444 shorter events, 76.3 us)
Async XLA Ops:
  8.0 446.8 %all-reduce.29.cloned.1.call-start = ((), (), s32[]{:S(2)}) async-start(), calls=%async_computation.4 | async-start | bytes 1228800 | tf_op jit(solution)/shard_map/psum | solution.py:90
  94.2 160.4 %copy-start.29 = (bf16[2,197,384]{2,0,1:T(2,128)(2,1)S(1)}, bf16[2,197,384]{2,0,1:T(2,128)(2,1)}, u32[]{:S(2)}) copy-start(bf16[2,197,384]{2,0,1:T(2,128)(2,1)} %param.18) | copy-start | bytes 907780
  96.1 239.6 %copy-start.52 = (f32[384]{0:T(512)}, f32[384]{0:T(512)S(1)}, u32[]{:S(2)}) copy-start(f32[384]{0:T(512)S(1)} %get-tuple-element.77) | copy-start | bytes 4612
  175.0 281.4 %copy-start.54 = (f32[384]{0:T(512)}, f32[384]{0:T(512)S(1)}, u32[]{:S(2)}) copy-start(f32[384]{0:T(512)S(1)} %get-tuple-element.74) | copy-start | bytes 4612
  254.6 84.0 %copy-start.5 = (bf16[1,192,384]{2,1,0:T(8,128)(2,1)}, bf16[1,192,384]{2,1,0:T(8,128)(2,1)S(1)}, u32[]{:S(2)}) copy-start(bf16[1,192,384]{2,1,0:T(8,128)(2,1)S(1)} %copy.158) | copy-start | bytes 442372
  255.2 80.6 %copy-start.58 = (f32[197]{0:T(256)}, f32[197]{0:T(256)S(1)}, u32[]{:S(2)}) copy-start(f32[197]{0:T(256)S(1)} %broadcast_multiply_fusion.11) | copy-start | bytes 2368
  255.4 80.4 %copy-start.66 = (f32[197]{0:T(256)}, f32[197]{0:T(256)S(1)}, u32[]{:S(2)}) copy-start(f32[197]{0:T(256)S(1)} %add_rsqrt_fusion.3) | copy-start | bytes 2368
  255.5 80.1 %copy-start.56 = (f32[197]{0:T(256)}, f32[197]{0:T(256)S(1)}, u32[]{:S(2)}) copy-start(f32[197]{0:T(256)S(1)} %broadcast_multiply_fusion.9) | copy-start | bytes 2368
  255.8 79.9 %copy-start.64 = (f32[197]{0:T(256)}, f32[197]{0:T(256)S(1)}, u32[]{:S(2)}) copy-start(f32[197]{0:T(256)S(1)} %add_rsqrt_fusion.1) | copy-start | bytes 2368
  337.7 11.9 copy-start.33
  339.6 124.3 %all-gather.10.cloned.1.call-start = ((), (), s32[]{:S(2)}) async-start(), calls=%async_computation | async-start | bytes 2396160 | tf_op jit(solution)/shard_map/all_gather | solution.py:53
  340.2 215.7 %all-gather.12.cloned.1.call-start = ((), (), s32[]{:S(2)}) async-start(), calls=%async_computation.1 | async-start | bytes 2396160 | tf_op jit(solution)/shard_map/all_gather | solution.py:54
  340.8 350.2 %all-reduce.27.cloned.1.call-start = ((), (), s32[]{:S(2)}) async-start(), calls=%async_computation.3 | async-start | bytes 1228800 | tf_op jit(solution)/shard_map/psum | solution.py:184
  359.2 7.8 copy-start.30
  360.3 7.9 copy-start.104
  363.4 100.3 %copy-start.96 = (pred[416]{0:T(512)(128)(4,1)}, pred[416]{0:T(512)(128)(4,1)S(1)}, u32[]{:S(2)}) copy-start(pred[416]{0:T(512)(128)(4,1)S(1)} %compare_and_fusion.3) | copy-start | bytes 1252
  366.4 96.5 %copy-start.95 = (pred[416]{0:T(512)(128)(4,1)}, pred[416]{0:T(512)(128)(4,1)S(1)}, u32[]{:S(2)}) copy-start(pred[416]{0:T(512)(128)(4,1)S(1)} %compare_and_fusion.1) | copy-start | bytes 1252
  367.4 79.7 %copy-start.7 = (bf16[1,197,384]{2,0,1:T(2,128)(2,1)}, bf16[1,197,384]{2,0,1:T(2,128)(2,1)S(1)}, u32[]{:S(2)}) copy-start(bf16[1,197,384]{2,0,1:T(2,128)(2,1)S(1)} %get-tuple-element.115) | copy-start | bytes 453892
  446.8 14.6 %copy-start.48 = (bf16[1,384,4]{1,2,0:T(4,128)(2,1)}, bf16[1,384,4]{1,2,0:T(4,128)(2,1)S(1)}, u32[]{:S(2)}) copy-start(bf16[1,384,4]{1,2,0:T(4,128)(2,1)S(1)} %copy.162) | copy-start | bytes 9220
  454.8 108.7 %copy-start.80 = (s32[1024]{0:T(1024)}, s32[1024]{0:T(1024)S(1)}, u32[]{:S(2)}) copy-start(s32[1024]{0:T(1024)S(1)} %pad_clamp_fusion.2) | copy-start | bytes 12292
  470.5 90.7 %copy-start.1 = (bf16[4,104,768]{2,1,0:T(8,128)(2,1)}, bf16[4,104,768]{2,1,0:T(8,128)(2,1)S(1)}, u32[]{:S(2)}) copy-start(bf16[4,104,768]{2,1,0:T(8,128)(2,1)S(1)} %fusion.35) | copy-start | bytes 1916932
  568.0 5.6 copy-start
  576.6 26.8 %copy-start.14 = (f32[416,384]{1,0:T(8,128)S(1)}, f32[416,384]{1,0:T(8,128)}, u32[]{:S(2)}) copy-start(f32[416,384]{1,0:T(8,128)} %gather_fusion.6) | copy-start | bytes 1916932
  611.3 12.8 copy-start.13
  655.1 258.3 %all-reduce.31.cloned.1.call-start = ((), (), s32[]{:S(2)}) async-start(), calls=%async_computation.5 | async-start | bytes 1228800 | tf_op jit(solution)/shard_map/psum | solution.py:113
  655.2 37.9 %copy-start.87 = (f32[197]{0:T(256)}, f32[197]{0:T(256)S(1)}, u32[]{:S(2)}) copy-start(f32[197]{0:T(256)S(1)} %multiply_reduce_fusion.14) | copy-start | bytes 2368
  655.3 35.8 %copy-start.89 = (f32[197]{0:T(256)}, f32[197]{0:T(256)S(1)}, u32[]{:S(2)}) copy-start(f32[197]{0:T(256)S(1)} %multiply_reduce_fusion.15) | copy-start | bytes 2368
  655.3 35.8 %copy-start.49 = (bf16[1,384,4]{1,2,0:T(4,128)(2,1)S(1)}, bf16[1,384,4]{1,2,0:T(4,128)(2,1)}, u32[]{:S(2)}) copy-start(bf16[1,384,4]{1,2,0:T(4,128)(2,1)} %copy-done.48) | copy-start | bytes 9220
  655.3 35.8 %copy-start.55 = (f32[384]{0:T(512)S(1)}, f32[384]{0:T(512)}, u32[]{:S(2)}) copy-start(f32[384]{0:T(512)} %copy-done.54) | copy-start | bytes 4612
  655.3 35.7 %copy-start.73 = (f32[197]{0:T(256)S(1)}, f32[197]{0:T(256)}, u32[]{:S(2)}) copy-start(f32[197]{0:T(256)} %copy-done.72) | copy-start | bytes 2368
  655.3 35.7 %copy-start.85 = (f32[197]{0:T(256)S(1)}, f32[197]{0:T(256)}, u32[]{:S(2)}) copy-start(f32[197]{0:T(256)} %copy-done.84) | copy-start | bytes 2368
  655.3 37.8 %copy-start.22 = (bf16[1,197,384]{2,0,1:T(2,128)(2,1)S(1)}, bf16[1,197,384]{2,0,1:T(2,128)(2,1)}, u32[]{:S(2)}) copy-start(bf16[1,197,384]{2,0,1:T(2,128)(2,1)} %copy-done.21) | copy-start | bytes 453892
  655.3 37.8 %copy-start.71 = (f32[197]{0:T(256)S(1)}, f32[197]{0:T(256)}, u32[]{:S(2)}) copy-start(f32[197]{0:T(256)} %copy-done.70) | copy-start | bytes 2368
  655.3 37.8 %copy-start.83 = (f32[197]{0:T(256)S(1)}, f32[197]{0:T(256)}, u32[]{:S(2)}) copy-start(f32[197]{0:T(256)} %copy-done.82) | copy-start | bytes 2368
  701.4 621.5 %all-reduce.25.cloned.1.call-start = ((), (), s32[]{:S(2)}) async-start(), calls=%async_computation.2 | async-start | bytes 21233664
  712.4 5.2 copy-start.53
  712.4 5.2 copy-start.59
  712.4 5.2 copy-start.67
  721.0 153.9 %copy-start.103 = (u32[128]{0:T(128)S(1)}, u32[128]{0:T(128)}, u32[]{:S(2)}) copy-start(u32[128]{0:T(128)} %constant.216) | copy-start | bytes 1540
  721.0 175.6 %copy-start.20 = (bf16[197,384]{1,0:T(8,128)(2,1)S(1)}, bf16[197,384]{1,0:T(8,128)(2,1)}, u32[]{:S(2)}) copy-start(bf16[197,384]{1,0:T(8,128)(2,1)} %copy-done.19) | copy-start | bytes 453892
  721.1 175.7 %copy-start.76 = (f32[197]{0:T(256)S(1)}, f32[197]{0:T(256)}, u32[]{:S(2)}) copy-start(f32[197]{0:T(256)} %copy-done.74) | copy-start | bytes 2368
  721.1 175.7 %copy-start.90 = (f32[197]{0:T(256)S(1)}, f32[197]{0:T(256)}, u32[]{:S(2)}) copy-start(f32[197]{0:T(256)} %copy-done.89) | copy-start | bytes 2368
  721.1 189.7 %copy-start.18 = (bf16[197,384]{1,0:T(8,128)(2,1)S(1)}, bf16[197,384]{1,0:T(8,128)(2,1)}, u32[]{:S(2)}) copy-start(bf16[197,384]{1,0:T(8,128)(2,1)} %copy-done.17) | copy-start | bytes 453892
  721.1 189.7 %copy-start.88 = (f32[197]{0:T(256)S(1)}, f32[197]{0:T(256)}, u32[]{:S(2)}) copy-start(f32[197]{0:T(256)} %copy-done.87) | copy-start | bytes 2368
  721.1 189.9 %copy-start.94 = (f32[384]{0:T(512)S(1)}, f32[384]{0:T(512)}, u32[]{:S(2)}) copy-start(f32[384]{0:T(512)} %get-tuple-element.64) | copy-start | bytes 4612
  721.1 189.9 %copy-start.92 = (f32[384]{0:T(512)S(1)}, f32[384]{0:T(512)}, u32[]{:S(2)}) copy-start(f32[384]{0:T(512)} %get-tuple-element.62) | copy-start | bytes 4612
  721.1 189.9 %copy-start.91 = (f32[384]{0:T(512)S(1)}, f32[384]{0:T(512)}, u32[]{:S(2)}) copy-start(f32[384]{0:T(512)} %get-tuple-element.72) | copy-start | bytes 4612
  721.1 189.9 %copy-start.93 = (f32[384]{0:T(512)S(1)}, f32[384]{0:T(512)}, u32[]{:S(2)}) copy-start(f32[384]{0:T(512)} %get-tuple-element.73) | copy-start | bytes 4612
  867.1 6.5 collective-permute-start.15
  868.4 8.4 collective-permute-start.14
  869.7 16.6 %collective-permute-start.13 = (f32[192,8]{0,1:T(8,128)S(1)}, f32[192,8]{0,1:T(8,128)S(1)}, u32[]{:S(2)}, u32[]{:S(2)}) collective-permute-start(f32[192,8]{0,1:T(8,128)S(1)} %fusion), channel_id=1, source_target_pairs={{0,28},{2,30},{4,32},{6,34},{8,36},{10,38},{12,40},{14,42},{16,44}... | collective-permute-start | bytes 18440
  871.0 17.5 %collective-permute-start.12 = (f32[192,8]{0,1:T(8,128)S(1)}, f32[192,8]{0,1:T(8,128)S(1)}, u32[]{:S(2)}, u32[]{:S(2)}) collective-permute-start(f32[192,8]{0,1:T(8,128)S(1)} %fusion), channel_id=1, source_target_pairs={{0,26},{2,28},{4,30},{6,32},{8,34},{10,36},{12,38},{14,40},{16,42}... | collective-permute-start | bytes 18440
  872.3 18.7 %collective-permute-start.11 = (f32[192,8]{0,1:T(8,128)S(1)}, f32[192,8]{0,1:T(8,128)S(1)}, u32[]{:S(2)}, u32[]{:S(2)}) collective-permute-start(f32[192,8]{0,1:T(8,128)S(1)} %fusion), channel_id=1, source_target_pairs={{0,24},{2,26},{4,28},{6,30},{8,32},{10,34},{12,36},{14,38},{16,40}... | collective-permute-start | bytes 18440
  873.6 21.2 %collective-permute-start.10 = (f32[192,8]{0,1:T(8,128)S(1)}, f32[192,8]{0,1:T(8,128)S(1)}, u32[]{:S(2)}, u32[]{:S(2)}) collective-permute-start(f32[192,8]{0,1:T(8,128)S(1)} %fusion), channel_id=1, source_target_pairs={{0,22},{2,24},{4,26},{6,28},{8,30},{10,32},{12,34},{14,36},{16,38}... | collective-permute-start | bytes 18440
  876.8 20.0 %collective-permute-start.9 = (f32[192,8]{0,1:T(8,128)S(1)}, f32[192,8]{0,1:T(8,128)S(1)}, u32[]{:S(2)}, u32[]{:S(2)}) collective-permute-start(f32[192,8]{0,1:T(8,128)S(1)} %fusion), channel_id=1, source_target_pairs={{0,20},{2,22},{4,24},{6,26},{8,28},{10,30},{12,32},{14,34},{16,36}... | collective-permute-start | bytes 18440
  886.4 13.1 collective-permute-start.8
  888.5 15.2 %collective-permute-start.7 = (f32[192,8]{0,1:T(8,128)S(1)}, f32[192,8]{0,1:T(8,128)S(1)}, u32[]{:S(2)}, u32[]{:S(2)}) collective-permute-start(f32[192,8]{0,1:T(8,128)S(1)} %fusion), channel_id=1, source_target_pairs={{0,16},{2,18},{4,20},{6,22},{8,24},{10,26},{12,28},{14,30},{16,32}... | collective-permute-start | bytes 18440
  891.0 14.3 %collective-permute-start.6 = (f32[192,8]{0,1:T(8,128)S(1)}, f32[192,8]{0,1:T(8,128)S(1)}, u32[]{:S(2)}, u32[]{:S(2)}) collective-permute-start(f32[192,8]{0,1:T(8,128)S(1)} %fusion), channel_id=1, source_target_pairs={{0,14},{2,16},{4,18},{6,20},{8,22},{10,24},{12,26},{14,28},{16,30}... | collective-permute-start | bytes 18440
  894.8 13.0 collective-permute-start.5
  896.9 14.1 %collective-permute-start.4 = (f32[192,8]{0,1:T(8,128)S(1)}, f32[192,8]{0,1:T(8,128)S(1)}, u32[]{:S(2)}, u32[]{:S(2)}) collective-permute-start(f32[192,8]{0,1:T(8,128)S(1)} %fusion), channel_id=1, source_target_pairs={{0,10},{2,12},{4,14},{6,16},{8,18},{10,20},{12,22},{14,24},{16,26}... | collective-permute-start | bytes 18440
  899.4 11.6 collective-permute-start.3
  903.7 7.3 collective-permute-start.2
  905.3 5.7 collective-permute-start.1
  907.8 3.5 collective-permute-start
  (64 other events, 166.1 us)
Sparse Core Ops, SparseCore 0:
  339.7 36.0 all-reduce.28
  655.2 35.7 all-reduce.26
  701.5 38.7 all-reduce.30
  742.9 579.9 all-reduce.24
Sparse Core Ops, SparseCore 1:
  341.8 108.7 all-gather.9
  452.2 103.6 all-gather.11
where the time goes:
time: 1340 us
  blocking collectives  833 us (62%)
  waiting for transfers between devices  243 us (18%)
  local copies, waits for them, and re-layouts  105 us (8%)
  matrix products  51.3 us (4%)
  starting transfers between devices  42.1 us (3%)
  other arithmetic  41.3 us (3%)
  between operations  19.2 us (1%)
    unnamed x2, blocking collectives  421 us
    unnamed x23, waiting for transfers between devices  128 us
    all_gather x1, waiting for transfers between devices, fetch_layer(): lax.all_gather(w_out[layer_index], 'dp', axis=2, tiled=True)  85.3 us
    all_gather x1, blocking collectives, fetch_layer(): lax.all_gather(ln_bias[layer_index], 'dp', axis=1, tiled=True)  83.9 us
    all_gather x1, blocking collectives, fetch_layer(): lax.all_gather(w_proj[layer_index], 'dp', axis=1, tiled=True)  78.9 us
    all_gather x1, blocking collectives, fetch_layer(): lax.all_gather(w_qkv[layer_index], 'dp', axis=0, tiled=True)  78.6 us
    all_gather x1, blocking collectives, fetch_layer(): lax.all_gather(w_router[layer_index], 'dp', axis=0, tiled=True)  78.4 us
    all_gather x1, blocking collectives, fetch_layer(): lax.all_gather(ln_gain[layer_index], 'dp', axis=1, tiled=True)  77 us
  transfers between devices with their start and end apart: 22, of which 4 were waited for; matrix products, arithmetic and copies ran while one was open for 17% of the time, Pallas kernels for 0%

commit v1 on v0

--- a/solution.py
+++ b/solution.py
@@ -48,7 +48,10 @@
 
 def fetch_layer(layer_index, w_qkv, w_proj, w_in, w_out, w_router, ln_gain, ln_bias):
     return (
-        lax.all_gather(w_qkv[layer_index], "dp", axis=0, tiled=True),
+        jnp.concatenate(
+            lax.all_to_all(jnp.stack([w_qkv[layer_index]] * lax.axis_size("dp")), "dp", 0, 0),
+            axis=0,
+        ),
         lax.all_gather(w_proj[layer_index], "dp", axis=1, tiled=True),
         lax.all_gather(w_in[layer_index], "dp", axis=1, tiled=True),
         lax.all_gather(w_out[layer_index], "dp", axis=2, tiled=True),

time: 1340 us -> 1280 us (0.955)
  blocking collectives: 833 us -> 754 us
    all_gather x1 -> x0, blocking collectives: 78.6 us -> none  [fetch_layer(): lax.all_gather(w_qkv[layer_index], 'dp', axis=0, tiled=True)]
  transfers between devices with their start and end apart: 22 -> 23, of which waited for: 4 -> 4; matrix products, arithmetic and copies ran while one was open for 17% -> 18% of each run, Pallas kernels for 0% -> 0%
where the time goes in v1:
time: 1280 us; the launch traced here: 1270 us
  blocking collectives  754 us (59%)
  waiting for transfers between devices  244 us (19%)
  local copies, waits for them, and re-layouts  104 us (8%)
  starting transfers between devices  51.9 us (4%)
  matrix products  51.3 us (4%)
  other arithmetic  41.3 us (3%)
  between operations  19.2 us (2%)
    unnamed x2, blocking collectives  422 us
    unnamed x23, waiting for transfers between devices  128 us
    all_gather x1, waiting for transfers between devices, fetch_layer(): lax.all_gather(w_out[layer_index], 'dp', axis=2, tiled=True)  86.3 us
    all_gather x1, blocking collectives, fetch_layer(): lax.all_gather(ln_bias[layer_index], 'dp', axis=1, tiled=True)  84.1 us
    all_gather x1, blocking collectives, fetch_layer(): lax.all_gather(w_proj[layer_index], 'dp', axis=1, tiled=True)  78.1 us
    all_gather x1, blocking collectives, fetch_layer(): lax.all_gather(w_router[layer_index], 'dp', axis=0, tiled=True)  77.8 us
    all_gather x1, blocking collectives, fetch_layer(): lax.all_gather(ln_gain[layer_index], 'dp', axis=1, tiled=True)  77.7 us
    unnamed x17, starting transfers between devices  41.6 us
  transfers between devices with their start and end apart: 23, of which 4 were waited for; matrix products, arithmetic and copies ran while one was open for 18% of the time, Pallas kernels for 0%

profile of v1, /device:TPU:0, one launch (start us, length us, event | category | flops | bytes accessed | tf_op | source)
XLA Modules:
  0.0 1265.8 jit_solution(18301074325375952698)
XLA Ops:
  9.7 9.9 all-to-all-start
  19.9 84.1 %all-gather.1 = bf16[1,2,384]{1,0,2:T(2,128)(2,1)S(1)} all-gather(bf16[1,2,6]{1,0,2:T(2,128)(2,1)S(1)} %copy.165), channel_id=3, replica_groups=mesh['dp'=64,'mp'=2] {'dp'}, dimensions={2}, use_global_device_ids=true | all-gather | bytes 1560 | tf_op jit(solution)/shard_map/all_gather | solution.py:60
  104.2 1.7 slice_reduce_fusion
  105.9 77.7 %all-gather = bf16[1,2,384]{1,0,2:T(2,128)(2,1)S(1)} all-gather(bf16[1,2,6]{1,0,2:T(2,128)(2,1)S(1)} %copy.164), channel_id=2, replica_groups=mesh['dp'=64,'mp'=2] {'dp'}, dimensions={2}, use_global_device_ids=true | all-gather | bytes 1560 | tf_op jit(solution)/shard_map/all_gather | solution.py:59
  183.9 1.7 slice_reduce_fusion.1
  185.6 78.1 %all-gather.2 = bf16[1,192,384]{1,0,2:T(2,128)(2,1)S(1)} all-gather(bf16[1,192,6]{1,0,2:T(2,128)(2,1)S(1)} %copy.170), channel_id=4, replica_groups=mesh['dp'=64,'mp'=2] {'dp'}, dimensions={2}, use_global_device_ids=true | all-gather | bytes 149760 | tf_op jit(solution)/shard_map/all_gather | solution.py:55
  274.8 5.9 gather_fusion.3
  284.4 5.9 gather_fusion
  291.5 2.9 scatter_custom_fusion
  294.5 2.9 scatter_custom_fusion.1
  298.7 77.8 %all-gather.3 = bf16[1,384,4]{2,0,1:T(2,128)(2,1)S(1)} all-gather(bf16[1,6,4]{2,0,1:T(2,128)(2,1)S(1)} %copy.174), channel_id=5, replica_groups=mesh['dp'=64,'mp'=2] {'dp'}, dimensions={1}, use_global_device_ids=true | all-gather | bytes 3120 | tf_op jit(solution)/shard_map/all_gather | solution.py:58
  379.7 2.6 gather_fusion.6
  382.3 2.2 gather_fusion.8
  386.5 2.2 gather_fusion.4
  388.8 2.2 gather_fusion.1
  393.7 2.6 fusion.89
  397.4 2.9 fusion.35
  400.3 86.3 %all-gather.11.cloned.1.call-done = bf16[1,4,768,384]{2,1,0,3:T(4,128)(2,1)} async-done(((bf16[1,4,768,6]{2,1,0,3:T(4,128)(2,1)}), bf16[1,4,768,384]{2,1,0,3:T(4,128)(2,1)}) %all-gather.11.cloned.1.call-update) | async-done | bytes 2359312 | tf_op jit(solution)/shard_map/all_gather | solution.py:57
  486.6 5.4 copy.182
  491.9 2.2 fusion.7
  494.2 2.2 gather_fusion.2
  496.5 2.1 multiply_reduce_fusion.3
  498.7 2.7 fusion.90
  501.4 2.9 fusion.38
  504.9 2.4 gather_fusion.5
  507.3 2.9 multiply_reduce_fusion.1
  511.7 15.0 %all-reduce.16 = (f32[197,2]{1,0:T(8,128)}, f32[197,2]{1,0:T(8,128)}) all-reduce(f32[197,2]{1,0:T(8,128)} %reduce_sum.430, f32[197,2]{1,0:T(8,128)S(1)} %reduce_sum.420), channel_id=1, replica_groups=mesh['dp'=64,'mp'=2] {'mp'}, use_global_device_ids=true, to_apply=%region_49.54 | all-reduce | flops 788 | bytes 6304 | tf_op jit(solution)/shard_map/psum | solution.py:187
  530.5 3.6 scatter_custom_fusion.2
  535.0 4.1 fusion.30
  539.0 2.9 fusion.200
  542.0 2.3 reshape.620
  544.3 1.6 copy.200
  545.8 2.5 multiply_reduce_fusion.5
  551.2 3.6 scatter_custom_fusion.3
  555.7 4.1 fusion.27
  561.0 2.6 multiply_reduce_fusion.4
  563.6 4.1 fusion.199
  568.6 2.4 gather_fusion.7
  573.4 2.5 reduce_sum.418
  575.9 2.7 fusion.9
  578.6 2.2 gather_fusion.9
  583.3 2.5 reduce_sum.428
  586.1 5.7 convolution_add_fusion.1
  591.8 30.0 %all-reduce.27.cloned.1.call-done = (f32[197,384]{1,0:T(8,128)}, f32[197,384]{1,0:T(8,128)}) async-done(((f32[197,384]{1,0:T(8,128)}, f32[197,384]{1,0:T(8,128)}), (f32[197,384]{1,0:T(8,128)}, f32[197,384]{1,0:T(8,128)})) %all-reduce.27.cloned.1.call-update) | async-done | bytes 605200 | tf_op jit(solution)/shard_map/psum | solution.py:187
  621.8 2.0 multiply_reduce_fusion.7
  623.8 2.1 multiply_reduce_fusion.6
  632.5 3.2 convolution_add_fusion
  635.7 7.5 copy.205
  643.2 5.2 copy.206
  649.1 1.5 convolution_add_fusion.2
  652.2 145.4 %fusion = f32[192,8]{0,1:T(8,128)S(1)} fusion(f32[192,384]{0,1:T(8,128)S(1)} %convolution_add_fusion.3), kind=kCustom, calls=%all-reduce-scatter | all-reduce-scatter fusion | flops 98305 | bytes 301568
  807.3 9.5 collective-permute-start.9
  816.8 2.2 collective-permute-start.8
  819.0 2.4 collective-permute-start.7
  821.4 3.8 collective-permute-start.6
  825.3 1.9 collective-permute-start.5
  827.3 2.5 collective-permute-start.4
  829.9 4.3 collective-permute-start.3
  834.2 1.6 collective-permute-start.2
  835.8 2.5 collective-permute-start.1
  838.3 2.9 collective-permute-start
  849.1 276.1 %all-reduce.14 = (f32[384,4]{0,1:T(4,128)S(1)}, f32[2,384]{1,0:T(2,128)S(1)}, f32[2,384]{1,0:T(2,128)S(1)}) all-reduce(f32[384,4]{0,1:T(4,128)S(1)} %convolution_add_fusion.6, f32[2,384]{1,0:T(2,128)S(1)} %maximum_add_fusion, f32[2,384]{1,0:T(2,128)S(1)} %maximum_add_fusion.1), channel_id=12, replica_groups=mesh['dp'=64,'mp'=2] {'dp'}, use_global_device_ids=true, to_apply=%region_62.67.clone | all-reduce | flops 3072 | bytes 24576
  1127.2 126.6 %all-reduce.25.cloned.1.call-done = (f32[384,3,192]{2,0,1:T(8,128)}, f32[4,384,768]{2,0,1:T(4,128)}, f32[4,768,384]{1,0,2:T(4,128)}) async-done(((f32[384,3,192]{2,0,1:T(8,128)}, f32[4,384,768]{2,0,1:T(4,128)}, f32[4,768,384]{1,0,2:T(4,128)}), (f32[384,3,192]{2,0,1:T(8,128)}, f32[4,384,768]{2,0,1:T(4,128)}, f32[4,768,384]{1,0,2:T(4,128)})) %all-reduce.25.cloned.1.call-update) | async-done | bytes 10321936
  1256.7 1.5 dynamic-slice_bitcast_fusion
  (445 shorter events, 74.9 us)
Async XLA Ops:
  8.0 11.6 copy-start.101
  8.0 11.7 copy-start.102
  8.0 11.8 copy-start.95
  9.7 255.9 %all-to-all-start = ((bf16[64,6,3,192]{3,1,2,0:T(8,128)(2,1)}), bf16[64,6,3,192]{3,1,2,0:T(8,128)(2,1)S(1)}, u32[]{:S(2)}, u32[]{:S(2)}) async-start(bf16[64,6,3,192]{3,1,2,0:T(8,128)(2,1)} %stack.87), calls=%async_computation | async-start | bytes 1572864 | tf_op jit(solution)/shard_map/all_to_all | solution.py:52
  19.6 365.0 %all-reduce.29.cloned.1.call-start = ((), (), s32[]{:S(2)}) async-start(), calls=%async_computation.5 | async-start | bytes 1228800 | tf_op jit(solution)/shard_map/psum | solution.py:93
  104.0 160.4 %copy-start.29 = (bf16[2,197,384]{2,0,1:T(2,128)(2,1)S(1)}, bf16[2,197,384]{2,0,1:T(2,128)(2,1)}, u32[]{:S(2)}) copy-start(bf16[2,197,384]{2,0,1:T(2,128)(2,1)} %param.18) | copy-start | bytes 907780
  105.9 160.9 %copy-start.48 = (f32[384]{0:T(512)}, f32[384]{0:T(512)S(1)}, u32[]{:S(2)}) copy-start(f32[384]{0:T(512)S(1)} %get-tuple-element.77) | copy-start | bytes 4612
  185.6 200.7 %copy-start.50 = (f32[384]{0:T(512)}, f32[384]{0:T(512)S(1)}, u32[]{:S(2)}) copy-start(f32[384]{0:T(512)S(1)} %get-tuple-element.74) | copy-start | bytes 4612
  264.4 5.3 copy-start.3
  268.8 11.9 copy-start.33
  270.7 122.9 %all-gather.9.cloned.1.call-start = ((), (), s32[]{:S(2)}) async-start(), calls=%async_computation.1 | async-start | bytes 2396160 | tf_op jit(solution)/shard_map/all_gather | solution.py:56
  271.3 215.3 %all-gather.11.cloned.1.call-start = ((), (), s32[]{:S(2)}) async-start(), calls=%async_computation.2 | async-start | bytes 2396160 | tf_op jit(solution)/shard_map/all_gather | solution.py:57
  271.9 349.9 %all-reduce.27.cloned.1.call-start = ((), (), s32[]{:S(2)}) async-start(), calls=%async_computation.4 | async-start | bytes 1228800 | tf_op jit(solution)/shard_map/psum | solution.py:187
  290.3 7.8 copy-start.30
  291.4 7.2 copy-start.100
  294.5 99.0 %copy-start.91 = (pred[416]{0:T(512)(128)(4,1)}, pred[416]{0:T(512)(128)(4,1)S(1)}, u32[]{:S(2)}) copy-start(pred[416]{0:T(512)(128)(4,1)S(1)} %compare_and_fusion.3) | copy-start | bytes 1252
  294.5 82.0 %copy-start.97 = (s32[394,1]{0,1:T(1,128)}, s32[394,1]{0,1:T(1,128)S(1)}, u32[]{:S(2)}) copy-start(s32[394,1]{0,1:T(1,128)S(1)} %compare_select_fusion.2) | copy-start | bytes 4732
  297.5 95.2 %copy-start.90 = (pred[416]{0:T(512)(128)(4,1)}, pred[416]{0:T(512)(128)(4,1)S(1)}, u32[]{:S(2)}) copy-start(pred[416]{0:T(512)(128)(4,1)S(1)} %compare_and_fusion.1) | copy-start | bytes 1252
  298.5 78.1 %copy-start.5 = (bf16[1,197,384]{2,0,1:T(2,128)(2,1)}, bf16[1,197,384]{2,0,1:T(2,128)(2,1)S(1)}, u32[]{:S(2)}) copy-start(bf16[1,197,384]{2,0,1:T(2,128)(2,1)S(1)} %get-tuple-element.115) | copy-start | bytes 453892
  298.5 78.3 %copy-start.21 = (bf16[1,197,384]{2,0,1:T(2,128)(2,1)}, bf16[1,197,384]{2,0,1:T(2,128)(2,1)S(1)}, u32[]{:S(2)}) copy-start(bf16[1,197,384]{2,0,1:T(2,128)(2,1)S(1)} %get-tuple-element.114) | copy-start | bytes 453892
  376.6 14.6 %copy-start.44 = (bf16[1,384,4]{1,2,0:T(4,128)(2,1)}, bf16[1,384,4]{1,2,0:T(4,128)(2,1)S(1)}, u32[]{:S(2)}) copy-start(bf16[1,384,4]{1,2,0:T(4,128)(2,1)S(1)} %copy.175) | copy-start | bytes 9220
  384.5 109.7 %copy-start.76 = (s32[1024]{0:T(1024)}, s32[1024]{0:T(1024)S(1)}, u32[]{:S(2)}) copy-start(s32[1024]{0:T(1024)S(1)} %pad_clamp_fusion.2) | copy-start | bytes 12292
  400.3 91.6 %copy-start.1 = (bf16[4,104,768]{2,1,0:T(8,128)(2,1)}, bf16[4,104,768]{2,1,0:T(8,128)(2,1)S(1)}, u32[]{:S(2)}) copy-start(bf16[4,104,768]{2,1,0:T(8,128)(2,1)S(1)} %fusion.35) | copy-start | bytes 1916932
  498.7 5.6 copy-start
  507.3 26.8 %copy-start.12 = (f32[416,384]{1,0:T(8,128)S(1)}, f32[416,384]{1,0:T(8,128)}, u32[]{:S(2)}) copy-start(f32[416,384]{1,0:T(8,128)} %gather_fusion.6) | copy-start | bytes 1916932
  542.0 12.8 %copy-start.11 = (f32[416,384]{1,0:T(8,128)S(1)}, f32[416,384]{1,0:T(8,128)}, u32[]{:S(2)}) copy-start(f32[416,384]{1,0:T(8,128)} %gather_fusion.8) | copy-start | bytes 1916932
  585.8 258.0 %all-reduce.31.cloned.1.call-start = ((), (), s32[]{:S(2)}) async-start(), calls=%async_computation.6 | async-start | bytes 1228800 | tf_op jit(solution)/shard_map/psum | solution.py:116
  585.9 37.9 %copy-start.82 = (f32[197]{0:T(256)}, f32[197]{0:T(256)S(1)}, u32[]{:S(2)}) copy-start(f32[197]{0:T(256)S(1)} %multiply_reduce_fusion.14) | copy-start | bytes 2368
  586.0 35.8 %copy-start.84 = (f32[197]{0:T(256)}, f32[197]{0:T(256)S(1)}, u32[]{:S(2)}) copy-start(f32[197]{0:T(256)S(1)} %multiply_reduce_fusion.15) | copy-start | bytes 2368
  586.0 35.8 %copy-start.45 = (bf16[1,384,4]{1,2,0:T(4,128)(2,1)S(1)}, bf16[1,384,4]{1,2,0:T(4,128)(2,1)}, u32[]{:S(2)}) copy-start(bf16[1,384,4]{1,2,0:T(4,128)(2,1)} %copy-done.44) | copy-start | bytes 9220
  586.0 35.7 %copy-start.51 = (f32[384]{0:T(512)S(1)}, f32[384]{0:T(512)}, u32[]{:S(2)}) copy-start(f32[384]{0:T(512)} %copy-done.50) | copy-start | bytes 4612
  586.0 35.7 %copy-start.69 = (f32[197]{0:T(256)S(1)}, f32[197]{0:T(256)}, u32[]{:S(2)}) copy-start(f32[197]{0:T(256)} %copy-done.68) | copy-start | bytes 2368
  586.0 35.7 %copy-start.81 = (f32[197]{0:T(256)S(1)}, f32[197]{0:T(256)}, u32[]{:S(2)}) copy-start(f32[197]{0:T(256)} %copy-done.80) | copy-start | bytes 2368
  586.0 37.8 %copy-start.22 = (bf16[1,197,384]{2,0,1:T(2,128)(2,1)S(1)}, bf16[1,197,384]{2,0,1:T(2,128)(2,1)}, u32[]{:S(2)}) copy-start(bf16[1,197,384]{2,0,1:T(2,128)(2,1)} %copy-done.21) | copy-start | bytes 453892
  586.1 37.8 %copy-start.67 = (f32[197]{0:T(256)S(1)}, f32[197]{0:T(256)}, u32[]{:S(2)}) copy-start(f32[197]{0:T(256)} %copy-done.66) | copy-start | bytes 2368
  586.1 37.8 %copy-start.79 = (f32[197]{0:T(256)S(1)}, f32[197]{0:T(256)}, u32[]{:S(2)}) copy-start(f32[197]{0:T(256)} %copy-done.78) | copy-start | bytes 2368
  632.2 621.5 %all-reduce.25.cloned.1.call-start = ((), (), s32[]{:S(2)}) async-start(), calls=%async_computation.3 | async-start | bytes 21233664
  643.2 5.2 copy-start.55
  651.5 153.9 %copy-start.99 = (u32[128]{0:T(128)S(1)}, u32[128]{0:T(128)}, u32[]{:S(2)}) copy-start(u32[128]{0:T(128)} %constant.216) | copy-start | bytes 1540
  651.5 175.6 %copy-start.18 = (bf16[197,384]{1,0:T(8,128)(2,1)S(1)}, bf16[197,384]{1,0:T(8,128)(2,1)}, u32[]{:S(2)}) copy-start(bf16[197,384]{1,0:T(8,128)(2,1)} %copy-done.17) | copy-start | bytes 453892
  651.5 175.6 %copy-start.72 = (f32[197]{0:T(256)S(1)}, f32[197]{0:T(256)}, u32[]{:S(2)}) copy-start(f32[197]{0:T(256)} %copy-done.70) | copy-start | bytes 2368
  651.5 175.6 %copy-start.85 = (f32[197]{0:T(256)S(1)}, f32[197]{0:T(256)}, u32[]{:S(2)}) copy-start(f32[197]{0:T(256)} %copy-done.84) | copy-start | bytes 2368
  651.5 189.7 %copy-start.16 = (bf16[197,384]{1,0:T(8,128)(2,1)S(1)}, bf16[197,384]{1,0:T(8,128)(2,1)}, u32[]{:S(2)}) copy-start(bf16[197,384]{1,0:T(8,128)(2,1)} %copy-done.15) | copy-start | bytes 453892
  651.6 189.7 %copy-start.83 = (f32[197]{0:T(256)S(1)}, f32[197]{0:T(256)}, u32[]{:S(2)}) copy-start(f32[197]{0:T(256)} %copy-done.82) | copy-start | bytes 2368
  651.6 189.9 %copy-start.89 = (f32[384]{0:T(512)S(1)}, f32[384]{0:T(512)}, u32[]{:S(2)}) copy-start(f32[384]{0:T(512)} %get-tuple-element.64) | copy-start | bytes 4612
  651.6 189.8 %copy-start.87 = (f32[384]{0:T(512)S(1)}, f32[384]{0:T(512)}, u32[]{:S(2)}) copy-start(f32[384]{0:T(512)} %get-tuple-element.62) | copy-start | bytes 4612
  651.6 189.9 %copy-start.86 = (f32[384]{0:T(512)S(1)}, f32[384]{0:T(512)}, u32[]{:S(2)}) copy-start(f32[384]{0:T(512)} %get-tuple-element.72) | copy-start | bytes 4612
  651.6 189.9 %copy-start.88 = (f32[384]{0:T(512)S(1)}, f32[384]{0:T(512)}, u32[]{:S(2)}) copy-start(f32[384]{0:T(512)} %get-tuple-element.73) | copy-start | bytes 4612
  797.6 6.5 collective-permute-start.15
  798.9 8.4 collective-permute-start.14
  800.2 16.6 %collective-permute-start.13 = (f32[192,8]{0,1:T(8,128)S(1)}, f32[192,8]{0,1:T(8,128)S(1)}, u32[]{:S(2)}, u32[]{:S(2)}) collective-permute-start(f32[192,8]{0,1:T(8,128)S(1)} %fusion), channel_id=1, source_target_pairs={{0,28},{2,30},{4,32},{6,34},{8,36},{10,38},{12,40},{14,42},{16,44}... | collective-permute-start | bytes 18440
  801.5 17.5 %collective-permute-start.12 = (f32[192,8]{0,1:T(8,128)S(1)}, f32[192,8]{0,1:T(8,128)S(1)}, u32[]{:S(2)}, u32[]{:S(2)}) collective-permute-start(f32[192,8]{0,1:T(8,128)S(1)} %fusion), channel_id=1, source_target_pairs={{0,26},{2,28},{4,30},{6,32},{8,34},{10,36},{12,38},{14,40},{16,42}... | collective-permute-start | bytes 18440
  802.8 18.7 %collective-permute-start.11 = (f32[192,8]{0,1:T(8,128)S(1)}, f32[192,8]{0,1:T(8,128)S(1)}, u32[]{:S(2)}, u32[]{:S(2)}) collective-permute-start(f32[192,8]{0,1:T(8,128)S(1)} %fusion), channel_id=1, source_target_pairs={{0,24},{2,26},{4,28},{6,30},{8,32},{10,34},{12,36},{14,38},{16,40}... | collective-permute-start | bytes 18440
  804.1 21.2 %collective-permute-start.10 = (f32[192,8]{0,1:T(8,128)S(1)}, f32[192,8]{0,1:T(8,128)S(1)}, u32[]{:S(2)}, u32[]{:S(2)}) collective-permute-start(f32[192,8]{0,1:T(8,128)S(1)} %fusion), channel_id=1, source_target_pairs={{0,22},{2,24},{4,26},{6,28},{8,30},{10,32},{12,34},{14,36},{16,38}... | collective-permute-start | bytes 18440
  807.3 20.0 %collective-permute-start.9 = (f32[192,8]{0,1:T(8,128)S(1)}, f32[192,8]{0,1:T(8,128)S(1)}, u32[]{:S(2)}, u32[]{:S(2)}) collective-permute-start(f32[192,8]{0,1:T(8,128)S(1)} %fusion), channel_id=1, source_target_pairs={{0,20},{2,22},{4,24},{6,26},{8,28},{10,30},{12,32},{14,34},{16,36}... | collective-permute-start | bytes 18440
  816.8 13.1 %collective-permute-start.8 = (f32[192,8]{0,1:T(8,128)S(1)}, f32[192,8]{0,1:T(8,128)S(1)}, u32[]{:S(2)}, u32[]{:S(2)}) collective-permute-start(f32[192,8]{0,1:T(8,128)S(1)} %fusion), channel_id=1, source_target_pairs={{0,18},{2,20},{4,22},{6,24},{8,26},{10,28},{12,30},{14,32},{16,34}... | collective-permute-start | bytes 18440
  819.0 15.2 %collective-permute-start.7 = (f32[192,8]{0,1:T(8,128)S(1)}, f32[192,8]{0,1:T(8,128)S(1)}, u32[]{:S(2)}, u32[]{:S(2)}) collective-permute-start(f32[192,8]{0,1:T(8,128)S(1)} %fusion), channel_id=1, source_target_pairs={{0,16},{2,18},{4,20},{6,22},{8,24},{10,26},{12,28},{14,30},{16,32}... | collective-permute-start | bytes 18440
  821.4 14.3 %collective-permute-start.6 = (f32[192,8]{0,1:T(8,128)S(1)}, f32[192,8]{0,1:T(8,128)S(1)}, u32[]{:S(2)}, u32[]{:S(2)}) collective-permute-start(f32[192,8]{0,1:T(8,128)S(1)} %fusion), channel_id=1, source_target_pairs={{0,14},{2,16},{4,18},{6,20},{8,22},{10,24},{12,26},{14,28},{16,30}... | collective-permute-start | bytes 18440
  825.3 13.0 %collective-permute-start.5 = (f32[192,8]{0,1:T(8,128)S(1)}, f32[192,8]{0,1:T(8,128)S(1)}, u32[]{:S(2)}, u32[]{:S(2)}) collective-permute-start(f32[192,8]{0,1:T(8,128)S(1)} %fusion), channel_id=1, source_target_pairs={{0,12},{2,14},{4,16},{6,18},{8,20},{10,22},{12,24},{14,26},{16,28}... | collective-permute-start | bytes 18440
  827.3 14.1 %collective-permute-start.4 = (f32[192,8]{0,1:T(8,128)S(1)}, f32[192,8]{0,1:T(8,128)S(1)}, u32[]{:S(2)}, u32[]{:S(2)}) collective-permute-start(f32[192,8]{0,1:T(8,128)S(1)} %fusion), channel_id=1, source_target_pairs={{0,10},{2,12},{4,14},{6,16},{8,18},{10,20},{12,22},{14,24},{16,26}... | collective-permute-start | bytes 18440
  829.9 11.6 collective-permute-start.3
  834.2 7.3 collective-permute-start.2
  835.8 5.7 collective-permute-start.1
  838.3 3.5 collective-permute-start
  (63 other events, 168.6 us)
Sparse Core Ops, SparseCore 0:
  270.8 35.4 all-reduce.28
  585.9 35.7 all-reduce.26
  632.3 38.7 all-reduce.30
  673.8 579.9 all-reduce.24
Sparse Core Ops, SparseCore 1:
  272.9 108.1 all-gather.8
  382.6 103.9 all-gather.10
